TPU v7x, 256 devices: a whole 4x4x8 slice. The times are simulated.
256 devices in a mesh: box: 64 (over x, z, core), blk: 4 (over y).
Axes of the slice: x: 4, y: 4, z: 8, core: 2. Of those that a mesh axis runs over, the one named last changes fastest.
Arguments:
- operator_map: float32 [64, 1536, 1536], P('box', 'blk'), may hold values from -0.5 to 2, as said below
- face_list: int32 [64, 256], replicated, may hold values from 0 to 1535, as said below
Outputs:
- merged: float32 [64, 1536, 3072], P('box', 'blk')
Inputs may be any that keep to these rules, and one draw needn't show every extreme that they name: `operator_map`: each box's map is symmetric; its diagonal lies in 1 to 2. Points 6 i + f and 6 j + f with the same f lie on one face: their entry is zero unless |i - j| is 1 or 2, and then lies in -0.245 to -0.12. Entries between points of different faces lie in -0.5 to 0.5. `face_list`: entry i of box b's list is 6 i + f_b with f_b from 0 to 5, so each list rises; boxes 2p and 2p + 1 list opposite faces, f = 2 a + 1 and f = 2 a, with one a from 0 to 2 for each pair, entry i of one facing entry i of the other.
All inputs are finite; a program needn't handle non-finite values.
Results may differ from a plain program's by a relative error of at most 0.0003.
Values sent between devices are 32-bit elements; how exact they have to be, the bound alone decides.
A program may use at most 64 MiB of HBM per device.

v0:
```python
import jax
import jax.numpy as jnp
from jax import lax
from jax.sharding import PartitionSpec as P


def from_partner(block, axis, apart):
    count = lax.axis_size(axis)
    route = []
    for low in range(count):
        high = low | 1 << apart
        if high != low and high < count:
            route += [(low, high), (high, low)]
    return lax.ppermute(block, axis, route)


def on_device(operator_map, face_list):
    blocks = lax.axis_size("blk")
    box_index = lax.axis_index("box")
    blk_index = lax.axis_index("blk")
    local_rows = operator_map[0]
    row_count = local_rows.shape[0]
    face_size = face_list.shape[1]
    per_block = face_size // blocks
    own_list = lax.dynamic_index_in_dim(face_list, box_index, 0, keepdims=False)
    sibling_index = jnp.bitwise_xor(box_index, 1)
    sibling_list = lax.dynamic_index_in_dim(face_list, sibling_index, 0, keepdims=False)
    local_list = (
        lax.dynamic_slice_in_dim(own_list, blk_index * per_block, per_block) - blk_index * row_count
    )
    picked = jnp.take(local_rows, local_list, axis=0)
    face_block = lax.all_gather(picked, "blk", axis=0, tiled=True)
    own_face = jnp.take(face_block, own_list, axis=1)
    is_lower = jnp.bitwise_and(box_index, 1) == 0
    coupling = jnp.take(local_rows, own_list, axis=1)
    sibling_block = from_partner(face_block, "box", 0)
    schur_sum = own_face + jnp.take(sibling_block, sibling_list, axis=1)
    factor = jnp.linalg.cholesky(schur_sum)
    lower_part = jnp.where(is_lower, face_block, sibling_block)
    upper_part = jnp.where(is_lower, sibling_block, face_block)
    weights = jax.scipy.linalg.cho_solve((factor, True), coupling.T).T
    correction = jnp.dot(
        weights,
        jnp.concatenate([lower_part, upper_part], axis=1),
        precision=lax.Precision.HIGHEST,
        preferred_element_type=jnp.float32,
    )
    blank_rows = jnp.zeros_like(local_rows)
    diagonal_part = jnp.concatenate(
        [jnp.where(is_lower, local_rows, blank_rows), jnp.where(is_lower, blank_rows, local_rows)],
        axis=1,
    )
    return (diagonal_part - correction)[None, :, :]


def solution(mesh):
    in_specs = (P("box", "blk", None), P())
    out_specs = P("box", "blk", None)
    return jax.shard_map(
        on_device, mesh=mesh, in_specs=in_specs, out_specs=out_specs, check_vma=False
    )
```

profile of v0, /device:TPU:1, one launch (start us, length us, event | category | flops | bytes accessed | tf_op | source)
XLA Modules:
  0.0 132.3 jit_solution(14960521785130965118)
XLA Ops:
  6.5 0.0 all-gather.2.cloned.1.call-start
  6.5 0.8 compare_and_fusion.2
  7.3 0.0 copy-start
  7.3 2.7 %gather_fusion = f32[64,1536]{1,0:T(8,128)S(1)} fusion(f32[384,1536]{1,0:T(8,128)} %bitcast.56, s32[1024]{0:T(1024)S(1)} %pad_clamp_fusion.3), kind=kCustom, calls=%fused_computation.2 | custom fusion | bytes 786688 | tf_op jit(solution)/shard_map/jit(_take)/gather | solution.py:31
  10.1 0.9 broadcast_select_fusion.5
  10.9 0.0 all-gather.2.cloned.1.call-update
  11.0 0.0 copy-done
  11.0 2.0 %copy.10 = f32[384,1536]{0,1:T(8,128)} copy(f32[384,1536]{1,0:T(8,128)S(1)} %bitcast.57) | data formatting | bytes 4718592 | tf_op jit(solution)/shard_map/squeeze | solution.py:21
  12.9 0.7 compare_select_fusion
  13.6 2.8 %gather_fusion.1 = f32[256,384]{1,0:T(8,128)S(1)} fusion(f32[384,1536]{0,1:T(8,128)} %copy.10, s32[1024]{0:T(1024)S(1)} %pad_clamp_fusion), kind=kCustom, calls=%fused_computation.3 | custom fusion | bytes 787456 | tf_op jit(solution)/shard_map/jit(_take)/gather | solution.py:35
  16.4 0.7 constant_dynamic-slice_fusion.1
  17.2 26.8 %all-gather.2.cloned.1.call-done = f32[256,1536]{1,0:T(8,128)} async-done(((f32[64,1536]{1,0:T(8,128)}), f32[256,1536]{1,0:T(8,128)}) %all-gather.2.cloned.1.call-update) | async-done | bytes 1572880 | tf_op jit(solution)/shard_map/all_gather | solution.py:32
  44.0 0.7 collective-permute-start
  44.7 0.1 broadcast_select_fusion.4
  44.8 2.9 %broadcast_select_fusion.1 = (f32[384,1536]{1,0:T(8,128)}, f32[384,1536]{1,0:T(8,128)}) fusion(pred[]{:T(512)S(6)} %eq.3, f32[1,384,1536]{2,1,0:T(8,128)S(1)} %copy-done), kind=kLoop, calls=%fused_computation.12 | loop fusion | flops 1179648 | bytes 7077889 | tf_op jit(solution)/shard_map/jit(_where)/select_n | solution.py:50
  47.7 1.9 %copy.7 = f32[256,1536]{0,1:T(8,128)S(1)} copy(f32[256,1536]{1,0:T(8,128)} %all-gather.2.cloned.1.call-done) | data formatting | bytes 3145728 | tf_op jit(solution)/shard_map/all_gather | solution.py:32
  49.6 1.0 gather_fusion.2
  50.5 0.0 collective-permute-done
  50.5 1.9 %copy.8 = f32[256,1536]{0,1:T(8,128)S(1)} copy(f32[256,1536]{1,0:T(8,128)} %collective-permute-done) | data formatting | bytes 3145728 | tf_op jit(solution)/shard_map/ppermute | solution.py:14
  52.4 1.0 gather_fusion.3
  53.4 0.1 bitcast_add_fusion.1
  53.5 0.1 copy.9
  53.7 11.7 %cholesky.50 = f32[128,128]{1,0:T(8,128)S(1)} custom-call(f32[128,128]{1,0:T(8,128)S(1)} %cholesky.118), custom_call_target="Cholesky" | custom-call | tf_op jit(solution)/shard_map/jit(cholesky)/cholesky | solution.py:38
  65.5 0.7 compare_reduce_fusion.1
  66.2 9.8 %custom-call.18 = f32[1,128,128]{1,2,0:T(8,128)S(1)} custom-call(f32[1,128,128]{2,1,0:T(8,128)S(1)} %get-tuple-element.35), custom_call_target="InvertDiagBlocksLowerTriangular" | custom-call | tf_op jit(solution)/shard_map/jit(cholesky)/cholesky | solution.py:38
  76.0 0.2 constant_dynamic-update-slice_fusion
  76.2 0.3 convolution_subtract_fusion.2
  76.5 0.0 copy-start.3
  76.5 11.9 %cholesky.105 = f32[128,128]{1,0:T(8,128)S(1)} custom-call(f32[128,128]{1,0:T(8,128)S(1)} %convolution_subtract_fusion.2), custom_call_target="Cholesky" | custom-call | tf_op jit(solution)/shard_map/jit(cholesky)/cholesky | solution.py:38
  88.4 0.6 compare_reduce_fusion
  90.3 0.1 triangular_solve.70
  90.4 4.1 %while.1 = (s32[]{:T(128)}, f32[256,256]{1,0:T(8,128)S(1)}, s32[2,2]{1,0:T(2,128)S(1)}, f32[2,128,128]{2,1,0:T(8,128)S(1)}, s32[]{:T(128)}) while((s32[]{:T(128)}, f32[256,256]{1,0:T(8,128)S(1)}, s32[2,2]{1,0:T(2,128)S(1)}, f32[2,128,128]{2,1,0:T(8,128)S(1)}, s32[]{:T(128)}) %tuple.28), condition=%wide.while_cond, body=%wide.while_body.sunk | while | flops 2 | bytes 131189 | solution.py:41
  90.4 0.7 fusion.29
  91.1 1.3 %bitcast_dynamic-update-slice_fusion.2 = f32[2,128,128]{2,1,0:T(8,128)S(1)} fusion(f32[2,128,128]{2,1,0:T(8,128)S(1)} %get-tuple-element.77, s32[]{:T(128)S(6)} %copy.16, f32[256,256]{1,0:T(8,128)S(1)} %get-tuple-element.80, s32[]{:T(128)} %bitcast.54, s32[]{:T(128)} %bitcast.55), kind=kLoop, calls=%fused_computation.4.clone.1 | loop fusion | bytes 131084 | tf_op jit(solution)/shard_map/jit(_cho_solve)/triangular_solve
  92.5 0.7 fusion.29
  93.1 1.3 %bitcast_dynamic-update-slice_fusion.2 = f32[2,128,128]{2,1,0:T(8,128)S(1)} fusion(f32[2,128,128]{2,1,0:T(8,128)S(1)} %get-tuple-element.77, s32[]{:T(128)S(6)} %copy.16, f32[256,256]{1,0:T(8,128)S(1)} %get-tuple-element.80, s32[]{:T(128)} %bitcast.54, s32[]{:T(128)} %bitcast.55), kind=kLoop, calls=%fused_computation.4.clone.1 | loop fusion | bytes 131084 | tf_op jit(solution)/shard_map/jit(_cho_solve)/triangular_solve
  94.5 19.7 %custom-call.19 = f32[2,128,128]{1,2,0:T(8,128)S(1)} custom-call(f32[2,128,128]{2,1,0:T(8,128)S(1)} %get-tuple-element.13), custom_call_target="InvertDiagBlocksLowerTriangular" | custom-call | tf_op jit(solution)/shard_map/jit(_cho_solve)/triangular_solve | solution.py:41
  114.2 0.4 fusion.8
  114.5 0.3 convolution_subtract_fusion.1
  114.9 0.4 fusion.15
  115.2 0.3 fusion.14
  115.6 0.4 convolution_subtract_fusion
  115.9 0.3 fusion.13
  116.3 0.0 copy-done.3
  116.3 0.0 copy-start.1
  116.3 0.0 copy-start.2
  116.3 1.8 %broadcast_select_fusion.3 = (f32[256,1536]{1,0:T(8,128)S(1)}, f32[256,1536]{1,0:T(8,128)S(1)}) fusion(f32[256,1536]{1,0:T(8,128)S(1)} %copy-done.3, f32[256,1536]{1,0:T(8,128)} %collective-permute-done, pred[]{:T(512)S(6)} %eq.3), kind=kLoop, calls=%fused_computation.17 | loop fusion | flops 786432 | bytes 6291457 | tf_op jit(solution)/shard_map/jit(_where)/select_n | solution.py:39
  118.1 0.3 copy-done.1
  118.4 0.7 copy-done.2
  119.1 6.4 %fusion = f32[1,384,3072]{2,1,0:T(8,128)} fusion(f32[384,1536]{1,0:T(8,128)S(1)} %copy-done.2, f32[384,1536]{1,0:T(8,128)S(1)} %copy-done.1, f32[256,1536]{1,0:T(8,128)S(1)} %get-tuple-element.29, f32[256,1536]{1,0:T(8,128)S(1)} %get-tuple-element.28, f32[128,384]{1,0:T(8,128)S(1)} %fusion.14, f32[128,384]{1,0:T(8,128)S(1)} %fusion.13), kind=kOutput, calls=%fused_computation.7 | convolution fusion | flops 3627122688 | bytes 12976128 | tf_op jit(solution)/shard_map/dot_general | solution.py:42
  (18 shorter events, 0.2 us)
Async XLA Ops:
  6.5 37.5 %all-gather.2.cloned.1.call-start = ((), (), s32[]{:S(2)}) async-start(), calls=%async_computation | async-start | bytes 1966080 | tf_op jit(solution)/shard_map/all_gather | solution.py:32
  7.3 3.6 %copy-start = (f32[1,384,1536]{2,1,0:T(8,128)S(1)}, f32[1,384,1536]{2,1,0:T(8,128)}, u32[]{:S(2)}) copy-start(f32[1,384,1536]{2,1,0:T(8,128)} %param.4) | copy-start | bytes 7077892
  44.0 6.5 %collective-permute-start = (f32[256,1536]{1,0:T(8,128)}, f32[256,1536]{1,0:T(8,128)}, u32[]{:S(2)}, u32[]{:S(2)}) collective-permute-start(f32[256,1536]{1,0:T(8,128)} %all-gather.2.cloned.1.call-done), channel_id=1, source_target_pairs={{0,4},{4,0},{8,12},{12,8},{16,20},{20,16},{24,28},{28,24},{32,36},... | collective-permute-start | bytes 4718600 | tf_op jit(solution)/shard_map/ppermute | solution.py:14
  76.5 39.7 %copy-start.3 = (f32[256,1536]{1,0:T(8,128)S(1)}, f32[256,1536]{1,0:T(8,128)}, u32[]{:S(2)}) copy-start(f32[256,1536]{1,0:T(8,128)} %all-gather.2.cloned.1.call-done) | copy-start | bytes 4718596
  116.3 2.1 %copy-start.1 = (f32[384,1536]{1,0:T(8,128)S(1)}, f32[384,1536]{1,0:T(8,128)}, u32[]{:S(2)}) copy-start(f32[384,1536]{1,0:T(8,128)} %get-tuple-element.30) | copy-start | bytes 7077892
  116.3 2.8 %copy-start.2 = (f32[384,1536]{1,0:T(8,128)S(1)}, f32[384,1536]{1,0:T(8,128)}, u32[]{:S(2)}) copy-start(f32[384,1536]{1,0:T(8,128)} %get-tuple-element.31) | copy-start | bytes 7077892
Sparse Core Ops, SparseCore 0:
  11.1 32.8 all-gather.1
where the time goes:
time: 133 us; the launch traced here: 132 us
  other arithmetic  61.8 us (46%)
  waiting for transfers between devices  26.9 us (20%)
  local copies, waits for them, and re-layouts  19.1 us (14%)
  between operations  14.9 us (11%)
  matrix products  8.89 us (7%)
    another operation x7, other arithmetic, on_device(): factor = jnp.linalg.cholesky(schur_sum)  34.8 us
    all_gather x1, waiting for transfers between devices, on_device(): face_block = lax.all_gather(picked, 'blk', axis=0, tiled=True)  26.8 us
    another operation x3, other arithmetic, on_device(): weights = jax.scipy.linalg.cho_solve((factor, True), coupling.T).T  19.7 us
    dot_general x1, matrix products, on_device(): jnp.dot(weights, jnp.concatenate([lower_part, upper_part], axis=1), preci...  6.37 us
    another operation x6, local copies, waits for them, and re-layouts  4.03 us
    select_n x1, other arithmetic, on_device(): jnp.where(is_lower, local_rows, blank_rows)  2.87 us
    gather x1, local copies, waits for them, and re-layouts, on_device(): coupling = jnp.take(local_rows, own_list, axis=1)  2.8 us
    gather x1, local copies, waits for them, and re-layouts, on_device(): picked = jnp.take(local_rows, local_list, axis=0)  2.71 us
  transfers between devices with their start and end apart: 2, of which 1 were waited for; matrix products, arithmetic and copies ran while one was open for 9% of the time, Pallas kernels for 0%

commit v1 on v0

--- a/solution.py
+++ b/solution.py
@@ -2,6 +2,11 @@
 import jax.numpy as jnp
 from jax import lax
 from jax.sharding import PartitionSpec as P
+
+
+def gather_by_exchange(x, axis, dim):
+    copies = jnp.concatenate([x] * lax.axis_size(axis), axis=dim)
+    return lax.all_to_all(copies, axis, dim, dim, tiled=True)
 
 
 def from_partner(block, axis, apart):
@@ -29,7 +34,7 @@
         lax.dynamic_slice_in_dim(own_list, blk_index * per_block, per_block) - blk_index * row_count
     )
     picked = jnp.take(local_rows, local_list, axis=0)
-    face_block = lax.all_gather(picked, "blk", axis=0, tiled=True)
+    face_block = gather_by_exchange(picked, "blk", 0)
     own_face = jnp.take(face_block, own_list, axis=1)
     is_lower = jnp.bitwise_and(box_index, 1) == 0
     coupling = jnp.take(local_rows, own_list, axis=1)

time: 133 us -> 119 us (0.89)
  waiting for transfers between devices: 26.9 us -> 12.3 us
  between operations: 14.9 us -> 1.53 us
  starting transfers between devices: 0.68 us -> 8.52 us
  matrix products: 8.89 us -> 12.4 us
  local copies, waits for them, and re-layouts: 19.1 us -> 21.1 us
    all_gather x1 -> x0, waiting for transfers between devices: 26.8 us -> none  [on_device(): face_block = lax.all_gather(picked, 'blk', axis=0, tiled=True)]
    all_to_all x0 -> x1, waiting for transfers between devices: none -> 12.3 us  [gather_by_exchange(): return lax.all_to_all(copies, axis, dim, dim, tiled=True)]
    all_to_all x0 -> x1, starting transfers between devices: none -> 5.13 us  [gather_by_exchange(): return lax.all_to_all(copies, axis, dim, dim, tiled=True)]
    dot_general x1, matrix products: 6.37 us -> 9.86 us  [on_device(): jnp.dot(weights, jnp.concatenate([lower_part, upper_part], axis=1), preci...]
    all_to_all x0 -> x1, local copies, waits for them, and re-layouts: none -> 3.01 us  [gather_by_exchange(): return lax.all_to_all(copies, axis, dim, dim, tiled=True)]
    ppermute x1, starting transfers between devices: 0.68 us -> 3.38 us  [from_partner(): return lax.ppermute(block, axis, route)]
    ppermute x1 -> x0, local copies, waits for them, and re-layouts: 1.87 us -> none  [from_partner(): return lax.ppermute(block, axis, route)]
    all_gather x1 -> x0, local copies, waits for them, and re-layouts: 1.87 us -> none  [on_device(): face_block = lax.all_gather(picked, 'blk', axis=0, tiled=True)]
  transfers between devices with their start and end apart: 2 -> 2, of which waited for: 1 -> 1; matrix products, arithmetic and copies ran while one was open for 9% -> 10% of each run, Pallas kernels for 0% -> 0%
where the time goes in v1:
time: 119 us; the launch traced here: 118 us
  other arithmetic  62.3 us (52%)
  local copies, waits for them, and re-layouts  21.1 us (18%)
  matrix products  12.4 us (10%)
  waiting for transfers between devices  12.3 us (10%)
  starting transfers between devices  8.52 us (7%)
  between operations  1.53 us (1%)
    another operation x7, other arithmetic, on_device(): factor = jnp.linalg.cholesky(schur_sum)  34.7 us
    another operation x3, other arithmetic, on_device(): weights = jax.scipy.linalg.cho_solve((factor, True), coupling.T).T  19.7 us
    all_to_all x1, waiting for transfers between devices, gather_by_exchange(): return lax.all_to_all(copies, axis, dim, dim, tiled=True)  12.3 us
    dot_general x1, matrix products, on_device(): jnp.dot(weights, jnp.concatenate([lower_part, upper_part], axis=1), preci...  9.86 us
    all_to_all x1, starting transfers between devices, gather_by_exchange(): return lax.all_to_all(copies, axis, dim, dim, tiled=True)  5.13 us
    another operation x6, local copies, waits for them, and re-layouts  3.99 us
    ppermute x1, starting transfers between devices, from_partner(): return lax.ppermute(block, axis, route)  3.38 us
    all_to_all x1, local copies, waits for them, and re-layouts, gather_by_exchange(): return lax.all_to_all(copies, axis, dim, dim, tiled=True)  3.01 us
  transfers between devices with their start and end apart: 2, of which 1 were waited for; matrix products, arithmetic and copies ran while one was open for 10% of the time, Pallas kernels for 0%

profile of v1, /device:TPU:1, one launch (start us, length us, event | category | flops | bytes accessed | tf_op | source)
XLA Modules:
  0.0 118.2 jit_solution(6652443066940548356)
XLA Ops:
  0.0 0.8 compare_and_fusion.2
  0.8 2.6 %gather_fusion = f32[64,1536]{1,0:T(8,128)S(1)} fusion(f32[384,1536]{1,0:T(8,128)} %bitcast.58, s32[1024]{0:T(1024)S(1)} %pad_clamp_fusion.3), kind=kCustom, calls=%fused_computation.2 | custom fusion | bytes 786688 | tf_op jit(solution)/shard_map/jit(_take)/gather | solution.py:36
  3.4 0.1 broadcast_select_fusion.5
  3.5 1.3 %pad_maximum_fusion = f32[256,1536]{1,0:T(8,128)} fusion(f32[64,1536]{1,0:T(8,128)S(1)} %broadcast_select_fusion.5), kind=kLoop, calls=%fused_computation.11 | loop fusion | flops 1179648 | bytes 1966080 | tf_op jit(solution)/shard_map/concatenate | solution.py:8
  4.8 0.0 copy-start
  4.8 5.1 %all-to-all-start = ((f32[4,64,1536]{2,1,0:T(8,128)}), f32[4,64,1536]{2,1,0:T(8,128)}, u32[]{:S(2)}, u32[]{:S(2)}) async-start(f32[4,64,1536]{2,1,0:T(8,128)} %bitcast.60), calls=%async_computation | async-start | bytes 3145728 | tf_op jit(solution)/shard_map/all_to_all | solution.py:9
  9.9 0.0 copy-done
  9.9 1.9 %copy.9 = f32[384,1536]{0,1:T(8,128)} copy(f32[384,1536]{1,0:T(8,128)S(1)} %bitcast.59) | data formatting | bytes 4718592 | tf_op jit(solution)/shard_map/squeeze | solution.py:26
  11.9 0.7 compare_select_fusion
  12.6 2.8 %gather_fusion.1 = f32[256,384]{1,0:T(8,128)S(1)} fusion(f32[384,1536]{0,1:T(8,128)} %copy.9, s32[1024]{0:T(1024)S(1)} %pad_clamp_fusion), kind=kCustom, calls=%fused_computation.3 | custom fusion | bytes 787456 | tf_op jit(solution)/shard_map/jit(_take)/gather | solution.py:40
  15.4 0.7 constant_dynamic-slice_fusion.1
  16.1 12.3 %all-to-all-done = f32[4,64,1536]{2,1,0:T(8,128)} async-done(((f32[4,64,1536]{2,1,0:T(8,128)}), f32[4,64,1536]{2,1,0:T(8,128)}, u32[]{:S(2)}, u32[]{:S(2)}) %all-to-all-start) | async-done | bytes 1572896 | tf_op jit(solution)/shard_map/all_to_all | solution.py:9
  28.4 3.0 %copy.6 = f32[256,1536]{0,1:T(8,128)} copy(f32[256,1536]{1,0:T(8,128)} %bitcast.6) | data formatting | bytes 3145728 | tf_op jit(solution)/shard_map/all_to_all | solution.py:9
  31.4 3.4 %collective-permute-start = (f32[256,1536]{0,1:T(8,128)}, f32[256,1536]{0,1:T(8,128)}, u32[]{:S(2)}, u32[]{:S(2)}) collective-permute-start(f32[256,1536]{0,1:T(8,128)} %copy.6), channel_id=1, source_target_pairs={{0,4},{4,0},{8,12},{12,8},{16,20},{20,16},{24,28},{28,24},{32,36},... | collective-permute-start | bytes 4718600 | tf_op jit(solution)/shard_map/ppermute | solution.py:19
  34.8 0.1 broadcast_select_fusion.4
  34.9 2.9 %broadcast_select_fusion.1 = (f32[384,1536]{1,0:T(8,128)}, f32[384,1536]{1,0:T(8,128)}) fusion(pred[]{:T(512)S(6)} %eq.3, f32[1,384,1536]{2,1,0:T(8,128)S(1)} %copy-done), kind=kLoop, calls=%fused_computation.13 | loop fusion | flops 1179648 | bytes 7077889 | tf_op jit(solution)/shard_map/jit(_where)/select_n | solution.py:55
  37.8 2.4 %gather_fusion.2 = f32[256,256]{1,0:T(8,128)S(1)} fusion(f32[256,1536]{0,1:T(8,128)} %copy.6, s32[1024]{0:T(1024)S(1)} %pad_clamp_fusion.2), kind=kCustom, calls=%fused_computation.clone | custom fusion | bytes 525312 | tf_op jit(solution)/shard_map/jit(_take)/gather | solution.py:38
  40.2 0.0 collective-permute-done
  40.2 2.4 %gather_fusion.3 = f32[256,256]{1,0:T(8,128)S(1)} fusion(f32[256,1536]{0,1:T(8,128)} %collective-permute-done, s32[1024]{0:T(1024)S(1)} %pad_clamp_fusion.1), kind=kCustom, calls=%fused_computation.1.clone | custom fusion | bytes 525312 | tf_op jit(solution)/shard_map/jit(_take)/gather | solution.py:42
  42.6 0.1 bitcast_add_fusion.1
  42.7 0.1 copy.8
  42.9 11.7 %cholesky.50 = f32[128,128]{1,0:T(8,128)S(1)} custom-call(f32[128,128]{1,0:T(8,128)S(1)} %cholesky.118), custom_call_target="Cholesky" | custom-call | tf_op jit(solution)/shard_map/jit(cholesky)/cholesky | solution.py:43
  54.7 0.7 compare_reduce_fusion.1
  55.3 9.8 %custom-call.18 = f32[1,128,128]{1,2,0:T(8,128)S(1)} custom-call(f32[1,128,128]{2,1,0:T(8,128)S(1)} %get-tuple-element.35), custom_call_target="InvertDiagBlocksLowerTriangular" | custom-call | tf_op jit(solution)/shard_map/jit(cholesky)/cholesky | solution.py:43
  65.2 0.2 constant_dynamic-update-slice_fusion
  65.4 0.3 convolution_subtract_fusion.2
  65.6 11.7 %cholesky.105 = f32[128,128]{1,0:T(8,128)S(1)} custom-call(f32[128,128]{1,0:T(8,128)S(1)} %convolution_subtract_fusion.2), custom_call_target="Cholesky" | custom-call | tf_op jit(solution)/shard_map/jit(cholesky)/cholesky | solution.py:43
  77.4 0.7 compare_reduce_fusion
  79.4 0.1 triangular_solve.70
  79.5 4.2 %while.1 = (s32[]{:T(128)}, f32[256,256]{1,0:T(8,128)S(1)}, s32[2,2]{1,0:T(2,128)S(1)}, f32[2,128,128]{2,1,0:T(8,128)S(1)}, s32[]{:T(128)}) while((s32[]{:T(128)}, f32[256,256]{1,0:T(8,128)S(1)}, s32[2,2]{1,0:T(2,128)S(1)}, f32[2,128,128]{2,1,0:T(8,128)S(1)}, s32[]{:T(128)}) %tuple.28), condition=%wide.while_cond, body=%wide.while_body.sunk | while | flops 2 | bytes 131189 | solution.py:46
  79.7 0.6 fusion.29
  80.3 1.4 %bitcast_dynamic-update-slice_fusion.2 = f32[2,128,128]{2,1,0:T(8,128)S(1)} fusion(f32[2,128,128]{2,1,0:T(8,128)S(1)} %get-tuple-element.77, s32[]{:T(128)S(6)} %copy.17, f32[256,256]{1,0:T(8,128)S(1)} %get-tuple-element.80, s32[]{:T(128)} %bitcast.56, s32[]{:T(128)} %bitcast.57), kind=kLoop, calls=%fused_computation.4.clone.1 | loop fusion | bytes 131084 | tf_op jit(solution)/shard_map/jit(_cho_solve)/triangular_solve
  81.7 0.6 fusion.29
  82.3 1.4 %bitcast_dynamic-update-slice_fusion.2 = f32[2,128,128]{2,1,0:T(8,128)S(1)} fusion(f32[2,128,128]{2,1,0:T(8,128)S(1)} %get-tuple-element.77, s32[]{:T(128)S(6)} %copy.17, f32[256,256]{1,0:T(8,128)S(1)} %get-tuple-element.80, s32[]{:T(128)} %bitcast.56, s32[]{:T(128)} %bitcast.57), kind=kLoop, calls=%fused_computation.4.clone.1 | loop fusion | bytes 131084 | tf_op jit(solution)/shard_map/jit(_cho_solve)/triangular_solve
  83.7 19.7 %custom-call.19 = f32[2,128,128]{1,2,0:T(8,128)S(1)} custom-call(f32[2,128,128]{2,1,0:T(8,128)S(1)} %get-tuple-element.13), custom_call_target="InvertDiagBlocksLowerTriangular" | custom-call | tf_op jit(solution)/shard_map/jit(_cho_solve)/triangular_solve | solution.py:46
  103.4 0.0 copy-start.1
  103.4 0.4 fusion.8
  103.8 0.3 convolution_subtract_fusion.1
  104.1 0.4 fusion.15
  104.5 0.3 fusion.14
  104.8 0.4 convolution_subtract_fusion
  105.2 0.3 fusion.13
  105.5 0.0 copy-done.1
  105.5 0.0 copy-start.2
  105.5 0.0 copy-start.3
  105.5 1.8 %broadcast_select_fusion.3 = (f32[256,1536]{0,1:T(8,128)S(1)}, f32[256,1536]{0,1:T(8,128)S(1)}) fusion(f32[256,1536]{0,1:T(8,128)S(1)} %copy-done.1, f32[256,1536]{0,1:T(8,128)} %collective-permute-done, pred[]{:T(512)S(6)} %eq.3), kind=kLoop, calls=%fused_computation.18 | loop fusion | flops 786432 | bytes 6291457 | tf_op jit(solution)/shard_map/jit(_where)/select_n | solution.py:44
  107.3 0.3 copy-done.2
  107.7 0.7 copy-done.3
  108.4 9.9 %fusion = f32[1,384,3072]{2,1,0:T(8,128)} fusion(f32[384,1536]{1,0:T(8,128)S(1)} %copy-done.3, f32[384,1536]{1,0:T(8,128)S(1)} %copy-done.2, f32[256,1536]{0,1:T(8,128)S(1)} %get-tuple-element.29, f32[256,1536]{0,1:T(8,128)S(1)} %get-tuple-element.28, f32[128,384]{1,0:T(8,128)S(1)} %fusion.14, f32[128,384]{1,0:T(8,128)S(1)} %fusion.13), kind=kOutput, calls=%fused_computation.7 | convolution fusion | flops 3627122688 | bytes 12976128 | tf_op jit(solution)/shard_map/dot_general | solution.py:47
  (18 shorter events, 0.2 us)
Async XLA Ops:
  4.8 5.1 %copy-start = (f32[1,384,1536]{2,1,0:T(8,128)S(1)}, f32[1,384,1536]{2,1,0:T(8,128)}, u32[]{:S(2)}) copy-start(f32[1,384,1536]{2,1,0:T(8,128)} %param.4) | copy-start | bytes 7077892
  4.8 23.6 %all-to-all-start = ((f32[4,64,1536]{2,1,0:T(8,128)}), f32[4,64,1536]{2,1,0:T(8,128)}, u32[]{:S(2)}, u32[]{:S(2)}) async-start(f32[4,64,1536]{2,1,0:T(8,128)} %bitcast.60), calls=%async_computation | async-start | bytes 3145728 | tf_op jit(solution)/shard_map/all_to_all | solution.py:9
  31.4 8.8 %collective-permute-start = (f32[256,1536]{0,1:T(8,128)}, f32[256,1536]{0,1:T(8,128)}, u32[]{:S(2)}, u32[]{:S(2)}) collective-permute-start(f32[256,1536]{0,1:T(8,128)} %copy.6), channel_id=1, source_target_pairs={{0,4},{4,0},{8,12},{12,8},{16,20},{20,16},{24,28},{28,24},{32,36},... | collective-permute-start | bytes 4718600 | tf_op jit(solution)/shard_map/ppermute | solution.py:19
  103.4 2.1 %copy-start.1 = (f32[256,1536]{0,1:T(8,128)S(1)}, f32[256,1536]{0,1:T(8,128)}, u32[]{:S(2)}) copy-start(f32[256,1536]{0,1:T(8,128)} %copy.6) | copy-start | bytes 4718596
  105.5 2.1 %copy-start.2 = (f32[384,1536]{1,0:T(8,128)S(1)}, f32[384,1536]{1,0:T(8,128)}, u32[]{:S(2)}) copy-start(f32[384,1536]{1,0:T(8,128)} %get-tuple-element.30) | copy-start | bytes 7077892
  105.5 2.8 %copy-start.3 = (f32[384,1536]{1,0:T(8,128)S(1)}, f32[384,1536]{1,0:T(8,128)}, u32[]{:S(2)}) copy-start(f32[384,1536]{1,0:T(8,128)} %get-tuple-element.31) | copy-start | bytes 7077892
